TPU v7x, 128 devices: a whole 4x4x4 slice. The times are simulated.
128 devices in a mesh: fx: 16 (over x, z), fy: 8 (over y, core).
Axes of the slice: x: 4, y: 4, z: 4, core: 2. Of those that a mesh axis runs over, the one named last changes fastest.
Arguments:
- fluid_state: float32 [5, 8, 2048, 1024], P(None, None, 'fx', 'fy'), may hold values from -0.3 to 2.8, as said below
- surface_points: float32 [16384, 3, 128], P(('fx', 'fy')), may hold values from 0 to 1
- surface_normals: float32 [16384, 3, 128], P(('fx', 'fy')), may hold values from -1 to 1
- owner_ids: int32 [16384, 1], P(('fx', 'fy')), may hold values from 0 to 127; in each aligned block of 128 rows (0 to 127, 128 to 255, ...) at most 2 rows name the same one
- support_ids: int32 [16384, 2], P(('fx', 'fy')), may hold values from 0 to 7
- struct_points: float32 [1024, 3, 128], P(('fx', 'fy')), may hold values from 0 to 1
- couplings: float32 [1024, 4, 128, 128], P(('fx', 'fy')), may hold values from 0.5 to 1
- coupling_pattern: int32 [1024, 4], P(('fx', 'fy')), may hold values from 0 to 7, as said below
- stiff_diagonal: float32 [1024, 128], P(('fx', 'fy')), may hold values from 1.05 to 1.6
- struct_load: float32 [1024, 3, 128], P(('fx', 'fy')), may hold values from -6 to 6
- predicted: float32 [1024, 3, 128], P(('fx', 'fy')), may hold values from -3 to 3
- hist_residual: float32 [8, 1024, 3, 128], P(None, ('fx', 'fy')), may hold values from -0.03 to 0.03
- hist_response: float32 [8, 1024, 3, 128], P(None, ('fx', 'fy')), may hold values from -6 to 6
Outputs:
- new_state: float32 [5, 8, 2048, 1024], P(None, None, 'fx', 'fy')
- next_estimate: float32 [1024, 3, 128], P(('fx', 'fy'))
- coupling_residual: float32 [1024, 3, 128], P(('fx', 'fy'))
Inputs may be any that keep to these rules, and one draw needn't show every extreme that they name: `fluid_state`: component 0 (density) lies in [0.8, 1.2], components 1 to 3 (momenta) in [-0.3, 0.3], component 4 (total energy) in [2.2, 2.8]. `owner_ids`: among the 128 surface blocks of one device (aligned blocks of rows), no owner is named by more than 2 of them. `support_ids`: local block numbers on the owner. For each device's 8 structure blocks and each column k, the entries coupling_pattern[., k] are a permutation of 0 to 7.
All inputs are finite; a program needn't handle non-finite values.
Results may differ from a plain program's by a relative error of at most 0.0003.
Values sent between devices are 32-bit elements; how exact they have to be, the bound alone decides.
No kernel may reach another device: no remote copies, remote signals or barrier semaphores. Data moves between devices by JAX's collectives and lax.ppermute only.
A program may use at most 192 MiB of HBM per device.

v0:
```python
import math
import jax
import jax.numpy as jnp
from jax import lax
from jax.sharding import PartitionSpec as P

CG_ITERS = 2
COUPLE = 2
TOP_PRECISION = lax.Precision.HIGHEST
STEP_RATIO = 0.12
WALL_SPEED = 0.5
WALL_GAIN = 0.5
LOAD_SCALE = 4.0
PRESSURE_REF = 0.98
RADIUS = 1.0


def with_halo(cells, sides, width):
    for axis, dim in sides:
        count = lax.axis_size(axis)
        head = lax.slice_in_dim(cells, 0, width, axis=dim)
        tail = lax.slice_in_dim(cells, cells.shape[dim] - width, cells.shape[dim], axis=dim)
        cells = jnp.concatenate(
            [
                lax.ppermute(tail, axis, [(i, (i + 1) % count) for i in range(count)]),
                cells,
                lax.ppermute(head, axis, [((i + 1) % count, i) for i in range(count)]),
            ],
            axis=dim,
        )
    return cells


def state_pressure(state):
    return 0.4 * (
        state[4]
        - 0.5 * (state[1] * state[1] + state[2] * state[2] + state[3] * state[3]) / state[0]
    )


def face_terms(state, momentum):
    density = state[0]
    velocity = state[momentum] / density
    pressure = state_pressure(state)
    flux = state * velocity
    flux = flux.at[momentum].add(pressure)
    flux = flux.at[4].add(pressure * velocity)
    speed = jnp.abs(velocity) + jnp.sqrt(1.4 * pressure / density)
    return (flux, speed)


def rusanov(left, right, left_flux, right_flux, left_speed, right_speed):
    return 0.5 * (left_flux + right_flux) - 0.5 * jnp.maximum(left_speed, right_speed) * (
        right - left
    )


def vertical_terms(state, wall):
    bottom = state[:, 0]
    ghost = bottom.at[3].set(2.0 * bottom[0] * wall - bottom[3])
    column = jnp.concatenate([ghost[:, None], state, state[:, -1:]], axis=1)
    flux, speed = face_terms(column, 3)
    faces = rusanov(column[:, :-1], column[:, 1:], flux[:, :-1], flux[:, 1:], speed[:-1], speed[1:])
    return faces[:, 1:] - faces[:, :-1]


def horizontal_terms(state):
    extended = with_halo(state, (("fx", 2), ("fy", 3)), 1)
    strip = extended[:, :, :, 1:-1]
    flux, speed = face_terms(strip, 1)
    faces = rusanov(
        strip[:, :, :-1],
        strip[:, :, 1:],
        flux[:, :, :-1],
        flux[:, :, 1:],
        speed[:, :-1],
        speed[:, 1:],
    )
    total = faces[:, :, 1:] - faces[:, :, :-1]
    strip = extended[:, :, 1:-1, :]
    flux, speed = face_terms(strip, 2)
    faces = rusanov(
        strip[:, :, :, :-1],
        strip[:, :, :, 1:],
        flux[:, :, :, :-1],
        flux[:, :, :, 1:],
        speed[:, :, :-1],
        speed[:, :, 1:],
    )
    return total + (faces[:, :, :, 1:] - faces[:, :, :, :-1])


def kernel_block(fluid_points, struct_nodes):
    squared = jnp.zeros((), jnp.float32)
    for axis in range(3):
        offset = fluid_points[..., axis, :, None] - struct_nodes[..., axis, None, :]
        squared = squared + offset * offset
    ratio = jnp.sqrt(squared) / RADIUS
    reach = jnp.maximum(1.0 - ratio, 0.0)
    return reach * reach * reach * reach * (4.0 * ratio + 1.0)


def owner_kernels(places, support, struct_points):
    rows = places.shape[0]
    points = places.shape[-1]
    spread = support.shape[1]
    group = math.gcd(rows, 16)

    def one_group(inputs):
        where, which = inputs
        return kernel_block(where[:, None], struct_points[which])

    kernels = lax.map(
        one_group, (places.reshape(-1, group, 3, points), support.reshape(-1, group, spread))
    )
    return kernels.reshape(rows, spread, points, points)


def owner_motion(kernels, support, field_values):
    return jnp.einsum("gkij,gkcj->gci", kernels, field_values[support], precision=TOP_PRECISION)


def owner_loads(kernels, support, blocks, traction):
    flux_terms = jnp.einsum("gkij,gci->gkcj", kernels, traction, precision=TOP_PRECISION)
    selector = (support[:, :, None] == jnp.arange(blocks, dtype=jnp.int32)[None, None, :]).astype(
        jnp.float32
    )
    return jnp.einsum("rke,rkcj->ecj", selector, flux_terms, precision=TOP_PRECISION)


def route_coords(geometry, support):
    moved_geometry, moved_support = (
        lax.all_to_all(geometry, ("fx", "fy"), split_axis=0, concat_axis=0, tiled=True),
        lax.all_to_all(support, ("fx", "fy"), split_axis=0, concat_axis=0, tiled=True),
    )
    return (moved_geometry, moved_support)


def route_field(values):
    return lax.all_to_all(values, ("fx", "fy"), split_axis=0, concat_axis=0, tiled=True)


def global_sums(values):
    return lax.psum(values, ("fx", "fy"))


def stiffness(field_values, couplings, sparsity_layout, selector, diagonal):
    blocks = field_values.shape[0]
    scale = 1.0 / (2.0 * couplings.shape[1] * couplings.shape[2])
    flux_terms = jnp.einsum("aosq,avs->aovq", couplings, field_values, precision=TOP_PRECISION)
    shipped = jnp.einsum("bke,bkdj->edj", selector, flux_terms, precision=TOP_PRECISION)
    stacked = jnp.concatenate([shipped, field_values], axis=0)
    extended = with_halo(stacked, ((("fx", "fy"), 0),), blocks)
    prior_iterate = extended[:blocks]
    later = extended[-blocks:]
    forward_pass = jnp.einsum(
        "hzwm,hzlm->hlw", couplings, prior_iterate[sparsity_layout], precision=TOP_PRECISION
    )
    return diagonal[:, None, :] * field_values - scale * (forward_pass + later)


def conjugate(start, rhs, operate):
    residual = rhs - operate(start)
    solution = start
    direction = residual
    norm_now = global_sums(jnp.stack([jnp.sum(residual * residual)]))[0]
    for count in range(CG_ITERS):
        image = operate(direction)
        alpha = norm_now / global_sums(jnp.stack([jnp.sum(direction * image)]))[0]
        solution = solution + alpha * direction
        residual = residual - alpha * image
        if count + 1 < CG_ITERS:
            norm_next = global_sums(jnp.stack([jnp.sum(residual * residual)]))[0]
            direction = residual + norm_next / norm_now * direction
            norm_now = norm_next
    return solution


def newton_update(response, gram, projected, responses):
    lower = jnp.linalg.cholesky(gram)
    middle = lax.linalg.triangular_solve(lower, projected[:, None], left_side=True, lower=True)
    weights = lax.linalg.triangular_solve(
        lower, middle, left_side=True, lower=True, transpose_a=True
    )[:, 0]
    return response - jnp.einsum("h,hbdp->bdp", weights, responses, precision=TOP_PRECISION)


def on_device(
    fluid_state,
    surface_points,
    surface_normals,
    owner_ids,
    support_ids,
    struct_points,
    couplings,
    coupling_pattern,
    stiff_diagonal,
    struct_load,
    predicted,
    hist_residual,
    hist_response,
):
    rows_fx = lax.axis_size("fx")
    rows_fy = lax.axis_size("fy")
    devices = rows_fx * rows_fy
    surface_count = owner_ids.shape[0]
    capacity = max(2, 2 * surface_count // devices)
    owners = owner_ids[:, 0]
    chosen = (owners[:, None] == jnp.arange(devices, dtype=jnp.int32)[None, :]).astype(jnp.int32)
    slots = owners * capacity + jnp.sum((jnp.cumsum(chosen, axis=0) - chosen) * chosen, axis=1)
    width = devices * capacity

    def pack(values):
        return jnp.zeros((width,) + values.shape[1:], values.dtype).at[slots].set(values)

    owner_geometry, owner_support = route_coords(pack(surface_points), pack(support_ids))
    kernels = owner_kernels(owner_geometry, owner_support, struct_points)
    blocks = couplings.shape[0]
    selector = (
        coupling_pattern[:, :, None] == jnp.arange(blocks, dtype=jnp.int32)[None, None, :]
    ).astype(jnp.float32)

    def operate(field_values):
        return stiffness(field_values, couplings, coupling_pattern, selector, stiff_diagonal)

    horizontal = horizontal_terms(fluid_state)
    estimate = predicted
    differences = hist_residual
    responses = hist_response
    last_residual = predicted
    last_response = predicted
    new_state = fluid_state
    residual = predicted
    for count in range(COUPLE):
        motion_slots = owner_motion(kernels, owner_support, estimate)
        motion = route_field(motion_slots)[slots]
        wall = WALL_SPEED * jnp.tanh(WALL_GAIN * jnp.sum(surface_normals * motion, axis=1))
        new_state = fluid_state - STEP_RATIO * (horizontal + vertical_terms(fluid_state, wall))
        pressure = state_pressure(new_state[:, 0])
        traction = -LOAD_SCALE * (pressure - PRESSURE_REF)[:, None, :] * surface_normals
        owner_traction = route_field(pack(traction))
        loads = owner_loads(kernels, owner_support, blocks, owner_traction)
        response = conjugate(estimate, struct_load + loads, operate)
        residual = response - estimate
        if count > 0:
            differences = jnp.concatenate(
                [differences[1:], (residual - last_residual)[None]], axis=0
            )
            responses = jnp.concatenate([responses[1:], (response - last_response)[None]], axis=0)
        last_residual = residual
        last_response = response
        gram = jnp.einsum("hbdp,gbdp->hg", differences, differences, precision=TOP_PRECISION)
        projected = jnp.einsum("hbdp,bdp->h", differences, residual, precision=TOP_PRECISION)
        totals = global_sums(jnp.concatenate([gram, projected[:, None]], axis=1))
        estimate = newton_update(response, totals[:, :-1], totals[:, -1], responses)
    return (new_state, estimate, residual)


def solution(mesh):
    placed = (
        P(None, None, "fx", "fy"),
        P(("fx", "fy"), None, None),
        P(("fx", "fy"), None, None),
        P(("fx", "fy"), None),
        P(("fx", "fy"), None),
        P(("fx", "fy"), None, None),
        P(("fx", "fy"), None, None, None),
        P(("fx", "fy"), None),
        P(("fx", "fy"), None),
        P(("fx", "fy"), None, None),
        P(("fx", "fy"), None, None),
        P(None, ("fx", "fy"), None, None),
        P(None, ("fx", "fy"), None, None),
    )
    return jax.shard_map(
        on_device,
        mesh=mesh,
        in_specs=placed,
        out_specs=(
            P(None, None, "fx", "fy"),
            P(("fx", "fy"), None, None),
            P(("fx", "fy"), None, None),
        ),
        check_vma=False,
    )
```

profile of v0, /device:TPU:1, one launch (start us, length us, event | category | flops | bytes accessed | tf_op | source)
XLA Modules:
  0.0 1005.2 jit_solution(8151141601063758827)
XLA Ops:
  6.5 11.5 %all-to-all-start = ((s32[128,2,2]{1,2,0:T(2,128)}), s32[128,2,2]{1,2,0:T(2,128)S(1)}, u32[]{:S(2)}, u32[]{:S(2)}) async-start(s32[128,2,2]{1,2,0:T(2,128)} %copy.261), calls=%async_computation | async-start | bytes 262144 | tf_op jit(solution)/shard_map/all_to_all | solution.py:134
  19.6 5.4 collective-permute-start.1
  32.7 12.5 %scatter_fusion = f32[256,3,128]{2,1,0:T(4,128)} fusion(f32[256,3,128]{2,1,0:T(4,128)} %broadcast.438.clone, s32[128]{0:T(128)S(1)} %fusion.166, f32[128,3,128]{2,1,0:T(4,128)S(1)} %copy.265), kind=kCustom, calls=%fused_computation.12 | custom fusion | bytes 590336 | tf_op jit(solution)/shard_map/scatter | solution.py:214
  45.2 15.0 %all-to-all-start.1 = ((f32[256,3,128]{2,1,0:T(4,128)}), f32[256,3,128]{2,1,0:T(4,128)}, u32[]{:S(2)}, u32[]{:S(2)}) async-start(f32[256,3,128]{2,1,0:T(4,128)} %scatter_fusion), calls=%async_computation.1 | async-start | bytes 1048576 | tf_op jit(solution)/shard_map/all_to_all | solution.py:133
  60.8 2.2 gather_fusion.1
  63.0 2.0 pad_maximum_fusion.12
  65.0 3.3 fusion.182
  70.4 3.3 copy.253
  75.3 3.9 copy.254
  79.2 2.4 broadcast_multiply_fusion.2
  84.7 2.4 fusion.13
  87.1 3.2 copy.255
  90.4 3.2 copy.256
  93.6 5.9 pad_maximum_fusion
  100.7 3.1 slice_multiply_fusion
  103.8 3.0 fusion.26
  108.1 2.7 fusion.25
  110.8 1.8 copy.268
  112.6 69.3 %while.20 = (s32[]{:T(128)}, f32[16,16,2,128,128]{4,3,2,1,0:T(8,128)}, f32[16,16,3,128]{3,1,2,0:T(8,128)}, s32[16,16,2]{1,0,2:T(8,128)S(1)}, f32[8,3,128]{2,1,0:T(4,128)S(1)}, /*index=5*/s32[]{:T(128)}) while((s32[]{:T(128)}, f32[16,16,2,128,128]{4,3,2,1,0:T(8,128)}, f32[16,16,3,128]{3,1,2,0:T(8,128)}, s32[16,16,2]{1,0,2:T(8,128)S(1)}, ...), condition=%wide.region_5.6_spmd, body=%wide.region_4.5_spmd.sunk | while | flops 8389730 | bytes 2471257 | solution.py:113
  114.2 2.8 fusion.215
  118.6 2.7 fusion.215
  122.9 2.7 fusion.215
  127.3 2.7 fusion.215
  131.6 2.7 fusion.215
  135.9 2.7 fusion.215
  140.3 2.7 fusion.215
  144.6 2.7 fusion.215
  148.9 2.8 fusion.215
  153.3 2.7 fusion.215
  157.6 2.7 fusion.215
  161.9 2.7 fusion.215
  166.3 2.7 fusion.215
  170.6 2.7 fusion.215
  174.9 2.7 fusion.215
  179.2 2.7 fusion.215
  182.0 32.0 %convolution_bitcast_fusion.3 = f32[256,3,128]{2,1,0:T(4,128)} fusion(f32[256,2,128,128]{3,2,1,0:T(8,128)} %bitcast.465, f32[256,2,3,128]{3,1,0,2:T(2,128)S(1)} %bitcast.471), kind=kOutput, calls=%fused_computation.76 | convolution fusion | flops 301989888 | bytes 34734080 | tf_op jit(solution)/shard_map/gkij,gkcj->gci/dot_general | solution.py:120
  213.9 10.2 %all-to-all-start.2 = ((f32[256,3,128]{2,1,0:T(4,128)}), f32[256,3,128]{2,1,0:T(4,128)}, u32[]{:S(2)}, u32[]{:S(2)}) async-start(f32[256,3,128]{2,1,0:T(4,128)} %convolution_bitcast_fusion.3), calls=%async_computation.2 | async-start | bytes 1048576 | tf_op jit(solution)/shard_map/all_to_all | solution.py:140
  224.2 11.7 %fusion.4 = f32[5,8,128,129]{3,2,1,0:T(8,128)} fusion(f32[5,8,130,1]{3,2,1,0:T(8,128)} %copy.255, f32[5,8,1,128]{3,2,1,0:T(1,128)S(1)} %bitcast.482, f32[5,8,128,128]{3,2,1,0:T(8,128)} %param.40, f32[5,8,1,128]{3,2,1,0:T(1,128)S(1)} %bitcast.487, f32[5,8,130,1]{3,2,1,0:T(8,128)} %copy.256, f32[5,8,128,130]{3,2,1,0:T(8,128)} %fusion.25, f32[8,128,129]{2,1,0:T(8,128)} %fusion.24), kind=kLoop, calls=%fused_computation.29 | loop fusion | flops 7265280 | bytes 11158144 | tf_op jit(solution)/shard_map/sub | solution.py:53
  240.2 2.1 pad_maximum_fusion.8
  248.5 2.5 fusion.20
  252.1 12.4 %scatter_fusion.1 = f32[256,3,128]{2,1,0:T(4,128)} fusion(f32[256,3,128]{2,1,0:T(4,128)} %broadcast.438.clone.1, s32[128]{0:T(128)S(1)} %fusion.166, f32[128,3,128]{2,1,0:T(4,128)S(1)} %copy.273), kind=kCustom, calls=%fused_computation.13 | custom fusion | bytes 590336 | tf_op jit(solution)/shard_map/scatter | solution.py:214
  264.5 9.2 all-to-all-start.3
  276.7 10.5 %all-to-all-done.3 = f32[256,3,128]{2,1,0:T(4,128)S(1)} async-done(((f32[256,3,128]{2,1,0:T(4,128)}), f32[256,3,128]{2,1,0:T(4,128)S(1)}, u32[]{:S(2)}, u32[]{:S(2)}) %all-to-all-start.3) | async-done | bytes 393248 | tf_op jit(solution)/shard_map/all_to_all | solution.py:140
  287.2 19.6 %convolution_bitcast_fusion.1 = f32[256,2,3,128]{3,2,1,0:T(4,128)S(1)} fusion(f32[256,2,128,128]{3,2,1,0:T(8,128)} %bitcast.466, f32[256,3,128]{2,1,0:T(4,128)S(1)} %all-to-all-done.3), kind=kOutput, calls=%fused_computation.74 | convolution fusion | flops 301989888 | bytes 34734080 | tf_op jit(solution)/shard_map/gkij,gci->gkcj/dot_general | solution.py:124
  314.2 71.7 %all-reduce.1 = (f32[1]{0:T(128)}, f32[1]{0:T(128)}) all-reduce(f32[1]{0:T(128)} %bitcast.55, f32[1]{0:T(128)} %bitcast.63), channel_id=1, replica_groups=mesh['fx'=16,'fy'=8] {'fx','fy'}, use_global_device_ids=true, to_apply=%region_9.10 | all-reduce | flops 2 | bytes 16 | tf_op jit(solution)/shard_map/psum | solution.py:144
  388.0 62.7 %psum.72 = f32[1]{0:T(128)} all-reduce(f32[1]{0:T(128)} %bitcast.65), channel_id=1, replica_groups=mesh['fx'=16,'fy'=8] {'fx','fy'}, use_global_device_ids=true, to_apply=%region_13.14 | all-reduce | flops 1 | bytes 8 | tf_op jit(solution)/shard_map/psum | solution.py:144
  459.2 70.4 %psum.73 = f32[1]{0:T(128)} all-reduce(f32[1]{0:T(128)} %bitcast.74), channel_id=1, replica_groups=mesh['fx'=16,'fy'=8] {'fx','fy'}, use_global_device_ids=true, to_apply=%region_15.16 | all-reduce | flops 1 | bytes 8 | tf_op jit(solution)/shard_map/psum | solution.py:144
  531.3 62.6 %psum.74 = f32[8,9]{0,1:T(8,128)S(1)} all-reduce(f32[8,9]{0,1:T(8,128)S(1)} %pad_maximum_fusion.17), channel_id=1, replica_groups=mesh['fx'=16,'fy'=8] {'fx','fy'}, use_global_device_ids=true, to_apply=%region_16.17 | all-reduce | flops 72 | bytes 576 | tf_op jit(solution)/shard_map/psum | solution.py:144
  597.1 2.1 gather_fusion.6
  599.2 31.6 %convolution_bitcast_fusion.2 = f32[256,3,128]{2,1,0:T(4,128)} fusion(f32[256,2,3,128]{3,2,1,0:T(4,128)S(1)} %bitcast.472, f32[256,2,128,128]{3,2,1,0:T(8,128)} %bitcast.467), kind=kOutput, calls=%fused_computation.75 | convolution fusion | flops 301989888 | bytes 34734080 | tf_op jit(solution)/shard_map/gkij,gkcj->gci/dot_general | solution.py:120
  630.9 5.4 all-to-all-start.4
  637.1 1.9 collective-permute-start.10
  639.1 10.9 %all-to-all-done.4 = f32[256,3,128]{2,1,0:T(4,128)S(1)} async-done(((f32[256,3,128]{2,1,0:T(4,128)}), f32[256,3,128]{2,1,0:T(4,128)S(1)}, u32[]{:S(2)}, u32[]{:S(2)}) %all-to-all-start.4) | async-done | bytes 393248 | tf_op jit(solution)/shard_map/all_to_all | solution.py:140
  653.6 2.1 pad_maximum_fusion.7
  664.4 12.4 %scatter_fusion.2 = f32[256,3,128]{2,1,0:T(4,128)} fusion(f32[256,3,128]{2,1,0:T(4,128)} %broadcast.438, s32[128]{0:T(128)S(1)} %copy-done.27, f32[128,3,128]{2,1,0:T(4,128)S(1)} %copy.296), kind=kCustom, calls=%fused_computation.14 | custom fusion | bytes 590336 | tf_op jit(solution)/shard_map/scatter | solution.py:214
  676.8 4.6 all-to-all-start.5
  686.7 8.3 all-to-all-done.5
  695.0 19.6 %convolution_bitcast_fusion = f32[256,2,3,128]{3,2,1,0:T(4,128)S(1)} fusion(f32[256,2,128,128]{3,2,1,0:T(8,128)} %bitcast.468, f32[256,3,128]{2,1,0:T(4,128)S(1)} %all-to-all-done.5), kind=kOutput, calls=%fused_computation.73 | convolution fusion | flops 301989888 | bytes 34734080 | tf_op jit(solution)/shard_map/gkij,gci->gkcj/dot_general | solution.py:124
  718.2 1.8 convolution_bitcast_fusion.11
  721.3 71.7 %all-reduce = (f32[1]{0:T(128)}, f32[1]{0:T(128)}) all-reduce(f32[1]{0:T(128)} %bitcast.119, f32[1]{0:T(128)} %bitcast.127), channel_id=1, replica_groups=mesh['fx'=16,'fy'=8] {'fx','fy'}, use_global_device_ids=true, to_apply=%region_22.26 | all-reduce | flops 2 | bytes 16 | tf_op jit(solution)/shard_map/psum | solution.py:144
  795.0 62.5 %psum.77 = f32[1]{0:T(128)} all-reduce(f32[1]{0:T(128)} %bitcast.129), channel_id=1, replica_groups=mesh['fx'=16,'fy'=8] {'fx','fy'}, use_global_device_ids=true, to_apply=%region_26.30 | all-reduce | flops 1 | bytes 8 | tf_op jit(solution)/shard_map/psum | solution.py:144
  858.9 1.9 collective-permute-start.14
  866.1 70.4 %psum.78 = f32[1]{0:T(128)} all-reduce(f32[1]{0:T(128)} %bitcast.138), channel_id=1, replica_groups=mesh['fx'=16,'fy'=8] {'fx','fy'}, use_global_device_ids=true, to_apply=%region_28.32 | all-reduce | flops 1 | bytes 8 | tf_op jit(solution)/shard_map/psum | solution.py:144
  938.5 62.6 %psum.79 = f32[8,9]{0,1:T(8,128)S(1)} all-reduce(f32[8,9]{0,1:T(8,128)S(1)} %pad_maximum_fusion.18), channel_id=1, replica_groups=mesh['fx'=16,'fy'=8] {'fx','fy'}, use_global_device_ids=true, to_apply=%region_29.33 | all-reduce | flops 72 | bytes 576 | tf_op jit(solution)/shard_map/psum | solution.py:144
  (382 shorter events, 117.0 us)
Async XLA Ops:
  0.6 24.4 %copy-start = (f32[8,4,128,128]{3,2,1,0:T(8,128)S(1)}, f32[8,4,128,128]{3,2,1,0:T(8,128)}, u32[]{:S(2)}) copy-start(f32[8,4,128,128]{3,2,1,0:T(8,128)} %param.46) | copy-start | bytes 6291460
  0.6 27.7 %copy-start.1 = (f32[8,3,128]{2,0,1:T(8,128)S(1)}, f32[8,3,128]{2,0,1:T(8,128)}, u32[]{:S(2)}) copy-start(f32[8,3,128]{2,0,1:T(8,128)} %param.50) | copy-start | bytes 36868
  0.7 26.2 %copy-start.20 = (s32[8,4]{0,1:T(4,128)S(1)}, s32[8,4]{0,1:T(4,128)}, u32[]{:S(2)}) copy-start(s32[8,4]{0,1:T(4,128)} %param.47) | copy-start | bytes 388
  0.7 30.9 %copy-start.18 = (f32[128,3,128]{2,0,1:T(8,128)S(1)}, f32[128,3,128]{2,0,1:T(8,128)}, u32[]{:S(2)}) copy-start(f32[128,3,128]{2,0,1:T(8,128)} %param.41) | copy-start | bytes 589828
  1.7 29.9 %copy-start.25 = (f32[8,3,128]{2,0,1:T(8,128)S(1)}, f32[8,3,128]{2,0,1:T(8,128)}, u32[]{:S(2)}) copy-start(f32[8,3,128]{2,0,1:T(8,128)} %param.45) | copy-start | bytes 36868
  3.3 248.8 %copy-start.26 = (s32[128]{0:T(128)}, s32[128]{0:T(128)S(1)}, u32[]{:S(2)}) copy-start(s32[128]{0:T(128)S(1)} %fusion.166) | copy-start | bytes 1540
  6.5 38.7 %all-to-all-start = ((s32[128,2,2]{1,2,0:T(2,128)}), s32[128,2,2]{1,2,0:T(2,128)S(1)}, u32[]{:S(2)}, u32[]{:S(2)}) async-start(s32[128,2,2]{1,2,0:T(2,128)} %copy.261), calls=%async_computation | async-start | bytes 262144 | tf_op jit(solution)/shard_map/all_to_all | solution.py:134
  19.6 43.4 %collective-permute-start.1 = (f32[5,8,1,128]{3,1,2,0:T(8,128)}, f32[5,8,1,128]{3,1,2,0:T(8,128)S(1)}, u32[]{:S(2)}, u32[]{:S(2)}) collective-permute-start(f32[5,8,1,128]{3,1,2,0:T(8,128)} %bitcast.176), channel_id=1, source_target_pairs={{8,0},{16,8},{24,16},{32,24},{40,32},{48,40},{56,48},{64,56},{72,6... | collective-permute-start | bytes 61448 | tf_op jit(solution)/shard_map/ppermute | solution.py:27
  25.0 38.0 %collective-permute-start = (f32[5,8,1,128]{3,1,2,0:T(8,128)}, f32[5,8,1,128]{3,1,2,0:T(8,128)S(1)}, u32[]{:S(2)}, u32[]{:S(2)}) collective-permute-start(f32[5,8,1,128]{3,1,2,0:T(8,128)} %bitcast.175), channel_id=1, source_target_pairs={{0,8},{8,16},{16,24},{24,32},{32,40},{40,48},{48,56},{56,64},{64,7... | collective-permute-start | bytes 61448 | tf_op jit(solution)/shard_map/ppermute | solution.py:25
  27.7 279.1 %collective-permute-start.5 = (f32[8,3,128]{2,0,1:T(8,128)}, f32[8,3,128]{2,0,1:T(8,128)}, u32[]{:S(2)}, u32[]{:S(2)}) collective-permute-start(f32[8,3,128]{2,0,1:T(8,128)} %convolution_bitcast_fusion.22), channel_id=1, source_target_pairs={{1,0},{2,1},{3,2},{4,3},{5,4},{6,5},{7,6},{8,7},{9,8},{10,9},{11,1... | collective-permute-start | bytes 36872 | tf_op jit(solution)/shard_map/ppermute | solution.py:27
  28.3 245.9 %collective-permute-start.4 = (f32[8,3,128]{2,1,0:T(4,128)S(1)}, f32[8,3,128]{2,1,0:T(4,128)S(1)}, u32[]{:S(2)}, u32[]{:S(2)}) collective-permute-start(f32[8,3,128]{2,1,0:T(4,128)S(1)} %copy.275), channel_id=1, source_target_pairs={{0,1},{1,2},{2,3},{3,4},{4,5},{5,6},{6,7},{7,8},{8,9},{9,10},{10,1... | collective-permute-start | bytes 36872 | tf_op jit(solution)/shard_map/ppermute | solution.py:25
  30.7 30.1 %copy-start.9 = (f32[5,1,128,128]{3,2,1,0:T(8,128)}, f32[5,1,128,128]{3,2,1,0:T(8,128)S(1)}, u32[]{:S(2)}) copy-start(f32[5,1,128,128]{3,2,1,0:T(8,128)S(1)} %get-tuple-element.226) | copy-start | bytes 983044
  30.7 206.5 %copy-start.28 = (s32[1024]{0:T(1024)}, s32[1024]{0:T(1024)S(1)}, u32[]{:S(2)}) copy-start(s32[1024]{0:T(1024)S(1)} %pad_clamp_fusion.2) | copy-start | bytes 12292
  45.2 65.6 %all-to-all-start.1 = ((f32[256,3,128]{2,1,0:T(4,128)}), f32[256,3,128]{2,1,0:T(4,128)}, u32[]{:S(2)}, u32[]{:S(2)}) async-start(f32[256,3,128]{2,1,0:T(4,128)} %scatter_fusion), calls=%async_computation.1 | async-start | bytes 1048576 | tf_op jit(solution)/shard_map/all_to_all | solution.py:133
  65.0 4.2 copy-start.5
  73.7 13.5 %collective-permute-start.2 = (f32[5,8,130,1]{2,1,3,0:T(8,128)S(1)}, f32[5,8,130,1]{2,1,3,0:T(8,128)}, u32[]{:S(2)}, u32[]{:S(2)}) collective-permute-start(f32[5,8,130,1]{2,1,3,0:T(8,128)S(1)} %copy.253), channel_id=1, source_target_pairs={{0,1},{1,2},{2,3},{3,4},{4,5},{5,6},{6,7},{7,0},{8,9},{9,10},{10,1... | collective-permute-start | bytes 62408 | tf_op jit(solution)/shard_map/ppermute | solution.py:25
  79.2 2.7 copy-start.6
  79.2 11.2 %collective-permute-start.3 = (f32[5,8,130,1]{2,1,3,0:T(8,128)}, f32[5,8,130,1]{2,1,3,0:T(8,128)}, u32[]{:S(2)}, u32[]{:S(2)}) collective-permute-start(f32[5,8,130,1]{2,1,3,0:T(8,128)} %copy.254), channel_id=1, source_target_pairs={{1,0},{2,1},{3,2},{4,3},{5,4},{6,5},{7,6},{0,7},{9,8},{10,9},{11,1... | collective-permute-start | bytes 62408 | tf_op jit(solution)/shard_map/ppermute | solution.py:27
  82.0 1.1 copy-start.12
  83.0 1.7 copy-start.2
  213.9 23.2 %all-to-all-start.2 = ((f32[256,3,128]{2,1,0:T(4,128)}), f32[256,3,128]{2,1,0:T(4,128)}, u32[]{:S(2)}, u32[]{:S(2)}) async-start(f32[256,3,128]{2,1,0:T(4,128)} %convolution_bitcast_fusion.3), calls=%async_computation.2 | async-start | bytes 1048576 | tf_op jit(solution)/shard_map/all_to_all | solution.py:140
  224.2 14.8 %copy-start.14 = (f32[128,3,128]{2,0,1:T(8,128)S(1)}, f32[128,3,128]{2,0,1:T(8,128)}, u32[]{:S(2)}) copy-start(f32[128,3,128]{2,0,1:T(8,128)} %param.42) | copy-start | bytes 589828
  224.2 15.1 %copy-start.10 = (f32[5,1,128,128]{3,2,1,0:T(8,128)S(1)}, f32[5,1,128,128]{3,2,1,0:T(8,128)}, u32[]{:S(2)}) copy-start(f32[5,1,128,128]{3,2,1,0:T(8,128)} %copy-done.9) | copy-start | bytes 983044
  242.3 1.7 copy-start.3
  245.1 2.2 slice-start
  245.5 2.7 copy-start.7
  245.5 3.0 slice-start.1
  251.0 22.8 %copy-start.16 = (f32[8,8,3,128]{3,1,2,0:T(8,128)S(1)}, f32[8,8,3,128]{3,1,2,0:T(8,128)}, u32[]{:S(2)}) copy-start(f32[8,8,3,128]{3,1,2,0:T(8,128)} %param.51) | copy-start | bytes 294916
  264.5 22.7 %all-to-all-start.3 = ((f32[256,3,128]{2,1,0:T(4,128)}), f32[256,3,128]{2,1,0:T(4,128)S(1)}, u32[]{:S(2)}, u32[]{:S(2)}) async-start(f32[256,3,128]{2,1,0:T(4,128)} %scatter_fusion.1), calls=%async_computation.3 | async-start | bytes 1048576 | tf_op jit(solution)/shard_map/all_to_all | solution.py:140
  274.3 32.6 %copy-start.23 = (s32[256,2]{0,1:T(2,128)}, s32[256,2]{0,1:T(2,128)S(1)}, u32[]{:S(2)}) copy-start(s32[256,2]{0,1:T(2,128)S(1)} %eq.26) | copy-start | bytes 6148
  276.7 30.1 %copy-start.19 = (f32[8,128]{1,0:T(8,128)S(1)}, f32[8,128]{1,0:T(8,128)}, u32[]{:S(2)}) copy-start(f32[8,128]{1,0:T(8,128)} %param.48) | copy-start | bytes 12292
  276.7 30.1 %copy-start.22 = (f32[8,3,128]{2,0,1:T(8,128)S(1)}, f32[8,3,128]{2,0,1:T(8,128)}, u32[]{:S(2)}) copy-start(f32[8,3,128]{2,0,1:T(8,128)} %param.49) | copy-start | bytes 36868
  308.0 2.5 collective-permute-start.6
  310.5 3.1 collective-permute-start.7
  312.9 283.9 %copy-start.17 = (f32[8,8,3,128]{3,1,2,0:T(8,128)S(1)}, f32[8,8,3,128]{3,1,2,0:T(8,128)}, u32[]{:S(2)}) copy-start(f32[8,8,3,128]{3,1,2,0:T(8,128)} %param.52) | copy-start | bytes 294916
  452.1 3.0 collective-permute-start.8
  455.1 3.4 collective-permute-start.9
  630.9 19.1 %all-to-all-start.4 = ((f32[256,3,128]{2,1,0:T(4,128)}), f32[256,3,128]{2,1,0:T(4,128)S(1)}, u32[]{:S(2)}, u32[]{:S(2)}) async-start(f32[256,3,128]{2,1,0:T(4,128)} %convolution_bitcast_fusion.2), calls=%async_computation.4 | async-start | bytes 1048576 | tf_op jit(solution)/shard_map/all_to_all | solution.py:140
  637.1 47.1 %collective-permute-start.10 = (f32[8,3,128]{2,0,1:T(8,128)S(1)}, f32[8,3,128]{2,0,1:T(8,128)S(1)}, u32[]{:S(2)}, u32[]{:S(2)}) collective-permute-start(f32[8,3,128]{2,0,1:T(8,128)S(1)} %bitcast_subtract_fusion.1), channel_id=1, source_target_pairs={{0,1},{1,2},{2,3},{3,4},{4,5},{5,6},{6,7},{7,8},{8,9},{9,10},{10,1... | collective-permute-start | bytes 36872 | tf_op jit(solution)/shard_map/ppermute | solution.py:25
  655.7 1.7 copy-start.4
  655.7 1.8 copy-start.11
  659.0 1.7 copy-start.8
  660.7 2.6 copy-start.15
  660.7 3.7 copy-start.27
  661.8 1.5 copy-start.13
  676.8 18.1 %all-to-all-start.5 = ((f32[256,3,128]{2,1,0:T(4,128)}), f32[256,3,128]{2,1,0:T(4,128)S(1)}, u32[]{:S(2)}, u32[]{:S(2)}) async-start(f32[256,3,128]{2,1,0:T(4,128)} %scatter_fusion.2), calls=%async_computation.5 | async-start | bytes 1048576 | tf_op jit(solution)/shard_map/all_to_all | solution.py:140
  682.8 31.9 %collective-permute-start.11 = (f32[8,3,128]{2,0,1:T(8,128)S(1)}, f32[8,3,128]{2,0,1:T(8,128)S(1)}, u32[]{:S(2)}, u32[]{:S(2)}) collective-permute-start(f32[8,3,128]{2,0,1:T(8,128)S(1)} %convolution_bitcast_fusion.18), channel_id=1, source_target_pairs={{1,0},{2,1},{3,2},{4,3},{5,4},{6,5},{7,6},{8,7},{9,8},{10,9},{11,1... | collective-permute-start | bytes 36872 | tf_op jit(solution)/shard_map/ppermute | solution.py:27
  686.7 28.0 %copy-start.24 = (s32[256,2]{0,1:T(2,128)S(1)}, s32[256,2]{0,1:T(2,128)}, u32[]{:S(2)}) copy-start(s32[256,2]{0,1:T(2,128)} %copy-done.23) | copy-start | bytes 6148
  715.1 2.5 collective-permute-start.12
  717.5 3.1 collective-permute-start.13
  720.0 284.1 %slice-start.2 = ((f32[8,8,3,128]{3,1,2,0:T(8,128)}), f32[7,8,3,128]{3,1,2,0:T(8,128)S(1)}, s32[]{:S(2)}) async-start(f32[8,8,3,128]{3,1,2,0:T(8,128)} %param.52), calls=%async_computation.8 | async-start | bytes 172032 | tf_op jit(solution)/shard_map/slice | solution.py:249
  858.9 3.2 collective-permute-start.14
  862.0 3.4 collective-permute-start.15
  937.8 67.2 %copy-start.21 = (f32[8,3,128]{2,0,1:T(8,128)}, f32[8,3,128]{2,0,1:T(8,128)S(1)}, u32[]{:S(2)}) copy-start(f32[8,3,128]{2,0,1:T(8,128)S(1)} %get-tuple-element.201) | copy-start | bytes 36868
where the time goes:
time: 1010 us
  blocking collectives  535 us (53%)
  matrix products  127 us (13%)
  local copies, waits for them, and re-layouts  113 us (11%)
  other arithmetic  113 us (11%)
  starting transfers between devices  74.2 us (7%)
  waiting for transfers between devices  34.2 us (3%)
    psum x8, blocking collectives, global_sums(): return lax.psum(values, ('fx', 'fy'))  535 us
    dot_general x2, matrix products, owner_motion(): jnp.einsum('gkij,gkcj->gci', kernels, field_values[support], precision=TO...  63.6 us
    dynamic_update_slice x16, other arithmetic, owner_kernels(): lax.map(one_group, (places.reshape(-1, group, 3, points), support.reshape...  43.5 us
    dot_general x2, matrix products, owner_loads(): jnp.einsum('gkij,gci->gkcj', kernels, traction, precision=TOP_PRECISION)  39.3 us
    scatter x4, local copies, waits for them, and re-layouts, pack(): jnp.zeros((width,) + values.shape[1:], values.dtype).at[slots].set(values)  38.3 us
    all_to_all x4, waiting for transfers between devices, route_field(): lax.all_to_all(values, ('fx', 'fy'), split_axis=0, concat_axis=0, tiled=T...  30.9 us
    all_to_all x4, starting transfers between devices, route_field(): lax.all_to_all(values, ('fx', 'fy'), split_axis=0, concat_axis=0, tiled=T...  29.5 us
  transfers between devices with their start and end apart: 22, of which 8 were waited for; matrix products, arithmetic and copies ran while one was open for 29% of the time, Pallas kernels for 0%

commit v1 on v0

--- a/solution.py
+++ b/solution.py
@@ -141,7 +141,7 @@
 
 
 def global_sums(values):
-    return lax.psum(values, ("fx", "fy"))
+    return lax.psum(lax.psum(values, "fy"), "fx")
 
 
 def stiffness(field_values, couplings, sparsity_layout, selector, diagonal):

time: 1010 us -> 917 us (0.908)
  blocking collectives: 535 us -> 416 us
  starting transfers between devices: 74.2 us -> 91.7 us
    psum x8 -> x16, blocking collectives: 535 us -> 416 us  [global_sums(): return lax.psum(lax.psum(values, 'fy'), 'fx')]
  transfers between devices with their start and end apart: 22 -> 22, of which waited for: 8 -> 6; matrix products, arithmetic and copies ran while one was open for 29% -> 32% of each run, Pallas kernels for 0% -> 0%
where the time goes in v1:
time: 917 us; the launch traced here: 902 us
  blocking collectives  416 us (45%)
  matrix products  127 us (14%)
  other arithmetic  113 us (12%)
  local copies, waits for them, and re-layouts  112 us (12%)
  starting transfers between devices  91.7 us (10%)
  waiting for transfers between devices  33.6 us (4%)
  between operations  9.94 us (1%)
    psum x16, blocking collectives, global_sums(): return lax.psum(lax.psum(values, 'fy'), 'fx')  416 us
    dot_general x2, matrix products, owner_motion(): jnp.einsum('gkij,gkcj->gci', kernels, field_values[support], precision=TO...  63.6 us
    dynamic_update_slice x16, other arithmetic, owner_kernels(): lax.map(one_group, (places.reshape(-1, group, 3, points), support.reshape...  43.5 us
    dot_general x2, matrix products, owner_loads(): jnp.einsum('gkij,gci->gkcj', kernels, traction, precision=TOP_PRECISION)  39.3 us
    scatter x4, local copies, waits for them, and re-layouts, pack(): jnp.zeros((width,) + values.shape[1:], values.dtype).at[slots].set(values)  38.3 us
    all_to_all x4, starting transfers between devices, route_field(): lax.all_to_all(values, ('fx', 'fy'), split_axis=0, concat_axis=0, tiled=T...  34.9 us
    all_to_all x4, waiting for transfers between devices, route_field(): lax.all_to_all(values, ('fx', 'fy'), split_axis=0, concat_axis=0, tiled=T...  32.2 us
    ppermute x8, starting transfers between devices, with_halo(): lax.ppermute(tail, axis, [(i, (i + 1) % count) for i in range(count)])  18.8 us
  transfers between devices with their start and end apart: 22, of which 6 were waited for; matrix products, arithmetic and copies ran while one was open for 32% of the time, Pallas kernels for 0%

profile of v1, /device:TPU:1, one launch (start us, length us, event | category | flops | bytes accessed | tf_op | source)
XLA Modules:
  0.0 902.4 jit_solution(14803173979326477713)
XLA Ops:
  6.5 11.5 %all-to-all-start = ((s32[128,2,2]{1,2,0:T(2,128)}), s32[128,2,2]{1,2,0:T(2,128)S(1)}, u32[]{:S(2)}, u32[]{:S(2)}) async-start(s32[128,2,2]{1,2,0:T(2,128)} %copy.261), calls=%async_computation | async-start | bytes 262144 | tf_op jit(solution)/shard_map/all_to_all | solution.py:134
  19.6 5.4 collective-permute-start.1
  32.5 12.5 %scatter_fusion = f32[256,3,128]{2,1,0:T(4,128)} fusion(f32[256,3,128]{2,1,0:T(4,128)} %broadcast.438.clone, s32[128]{0:T(128)S(1)} %fusion.166, f32[128,3,128]{2,1,0:T(4,128)S(1)} %copy.265), kind=kCustom, calls=%fused_computation.12 | custom fusion | bytes 590336 | tf_op jit(solution)/shard_map/scatter | solution.py:214
  45.0 14.9 %all-to-all-start.1 = ((f32[256,3,128]{2,1,0:T(4,128)}), f32[256,3,128]{2,1,0:T(4,128)}, u32[]{:S(2)}, u32[]{:S(2)}) async-start(f32[256,3,128]{2,1,0:T(4,128)} %scatter_fusion), calls=%async_computation.1 | async-start | bytes 1048576 | tf_op jit(solution)/shard_map/all_to_all | solution.py:133
  64.7 3.3 fusion.182
  70.1 3.3 copy.253
  75.0 3.9 copy.254
  84.4 2.4 fusion.13
  86.9 3.2 copy.255
  90.1 3.2 copy.256
  93.3 5.9 pad_maximum_fusion
  100.4 3.1 slice_multiply_fusion
  103.5 3.0 fusion.26
  107.8 2.7 fusion.25
  112.3 69.4 %while.20 = (s32[]{:T(128)}, f32[16,16,2,128,128]{4,3,2,1,0:T(8,128)}, f32[16,16,3,128]{3,1,2,0:T(8,128)}, s32[16,16,2]{1,0,2:T(8,128)S(1)}, f32[8,3,128]{2,1,0:T(4,128)S(1)}, /*index=5*/s32[]{:T(128)}) while((s32[]{:T(128)}, f32[16,16,2,128,128]{4,3,2,1,0:T(8,128)}, f32[16,16,3,128]{3,1,2,0:T(8,128)}, s32[16,16,2]{1,0,2:T(8,128)S(1)}, ...), condition=%wide.region_5.6_spmd, body=%wide.region_4.5_spmd.sunk | while | flops 8389730 | bytes 2471257 | solution.py:113
  114.0 2.8 fusion.215
  118.3 2.7 fusion.215
  122.7 2.7 fusion.215
  127.0 2.7 fusion.215
  131.3 2.7 fusion.215
  135.7 2.7 fusion.215
  140.0 2.7 fusion.215
  144.3 2.7 fusion.215
  148.6 2.8 fusion.215
  153.0 2.7 fusion.215
  157.4 2.7 fusion.215
  161.7 2.7 fusion.215
  166.0 2.7 fusion.215
  170.3 2.7 fusion.215
  174.7 2.7 fusion.215
  179.0 2.7 fusion.215
  181.7 32.0 %convolution_bitcast_fusion.3 = f32[256,3,128]{2,1,0:T(4,128)} fusion(f32[256,2,128,128]{3,2,1,0:T(8,128)} %bitcast.465, f32[256,2,3,128]{3,1,0,2:T(2,128)S(1)} %bitcast.471), kind=kOutput, calls=%fused_computation.76 | convolution fusion | flops 301989888 | bytes 34734080 | tf_op jit(solution)/shard_map/gkij,gkcj->gci/dot_general | solution.py:120
  213.7 10.2 %all-to-all-start.2 = ((f32[256,3,128]{2,1,0:T(4,128)}), f32[256,3,128]{2,1,0:T(4,128)}, u32[]{:S(2)}, u32[]{:S(2)}) async-start(f32[256,3,128]{2,1,0:T(4,128)} %convolution_bitcast_fusion.3), calls=%async_computation.2 | async-start | bytes 1048576 | tf_op jit(solution)/shard_map/all_to_all | solution.py:140
  224.0 11.7 %fusion.4 = f32[5,8,128,129]{3,2,1,0:T(8,128)} fusion(f32[5,8,130,1]{3,2,1,0:T(8,128)} %copy.255, f32[5,8,1,128]{3,2,1,0:T(1,128)S(1)} %bitcast.482, f32[5,8,128,128]{3,2,1,0:T(8,128)} %param.40, f32[5,8,1,128]{3,2,1,0:T(1,128)S(1)} %bitcast.487, f32[5,8,130,1]{3,2,1,0:T(8,128)} %copy.256, f32[5,8,128,130]{3,2,1,0:T(8,128)} %fusion.25, f32[8,128,129]{2,1,0:T(8,128)} %fusion.24), kind=kLoop, calls=%fused_computation.29 | loop fusion | flops 7265280 | bytes 11158144 | tf_op jit(solution)/shard_map/sub | solution.py:53
  248.3 2.5 fusion.20
  251.8 12.5 %scatter_fusion.1 = f32[256,3,128]{2,1,0:T(4,128)} fusion(f32[256,3,128]{2,1,0:T(4,128)} %broadcast.438.clone.1, s32[128]{0:T(128)S(1)} %fusion.166, f32[128,3,128]{2,1,0:T(4,128)S(1)} %copy.273), kind=kCustom, calls=%fused_computation.13 | custom fusion | bytes 590336 | tf_op jit(solution)/shard_map/scatter | solution.py:214
  264.3 9.2 %all-to-all-start.3 = ((f32[256,3,128]{2,1,0:T(4,128)}), f32[256,3,128]{2,1,0:T(4,128)S(1)}, u32[]{:S(2)}, u32[]{:S(2)}) async-start(f32[256,3,128]{2,1,0:T(4,128)} %scatter_fusion.1), calls=%async_computation.3 | async-start | bytes 1048576 | tf_op jit(solution)/shard_map/all_to_all | solution.py:140
  276.2 10.6 %all-to-all-done.3 = f32[256,3,128]{2,1,0:T(4,128)S(1)} async-done(((f32[256,3,128]{2,1,0:T(4,128)}), f32[256,3,128]{2,1,0:T(4,128)S(1)}, u32[]{:S(2)}, u32[]{:S(2)}) %all-to-all-start.3) | async-done | bytes 393248 | tf_op jit(solution)/shard_map/all_to_all | solution.py:140
  286.9 19.6 %convolution_bitcast_fusion.1 = f32[256,2,3,128]{3,2,1,0:T(4,128)S(1)} fusion(f32[256,2,128,128]{3,2,1,0:T(8,128)} %bitcast.466, f32[256,3,128]{2,1,0:T(4,128)S(1)} %all-to-all-done.3), kind=kOutput, calls=%fused_computation.74 | convolution fusion | flops 301989888 | bytes 34734080 | tf_op jit(solution)/shard_map/gkij,gci->gkcj/dot_general | solution.py:124
  313.9 19.0 %all-reduce.3 = (f32[1]{0:T(128)}, f32[1]{0:T(128)}) all-reduce(f32[1]{0:T(128)} %bitcast.55, f32[1]{0:T(128)} %bitcast.63), channel_id=1, replica_groups=mesh['fx'=16,'fy'=8] {'fy'}, use_global_device_ids=true, to_apply=%region_9.10 | all-reduce | flops 2 | bytes 16 | tf_op jit(solution)/shard_map/psum | solution.py:144
  333.0 32.7 %all-reduce.1 = (f32[1]{0:T(128)}, f32[1]{0:T(128)}) all-reduce(f32[1]{0:T(128)} %get-tuple-element.200, f32[1]{0:T(128)} %get-tuple-element.201), channel_id=1, replica_groups=mesh['fx'=16,'fy'=8] {'fx'}, use_global_device_ids=true, to_apply=%region_10.11 | all-reduce | flops 2 | bytes 16 | tf_op jit(solution)/shard_map/psum | solution.py:144
  367.6 23.1 %psum.144 = f32[1]{0:T(128)} all-reduce(f32[1]{0:T(128)} %bitcast.65), channel_id=1, replica_groups=mesh['fx'=16,'fy'=8] {'fy'}, use_global_device_ids=true, to_apply=%region_15.16 | all-reduce | flops 1 | bytes 8 | tf_op jit(solution)/shard_map/psum | solution.py:144
  390.7 29.2 %psum.145 = f32[1]{0:T(128)} all-reduce(f32[1]{0:T(128)} %psum.144), channel_id=1, replica_groups=mesh['fx'=16,'fy'=8] {'fx'}, use_global_device_ids=true, to_apply=%region_16.17 | all-reduce | flops 1 | bytes 8 | tf_op jit(solution)/shard_map/psum | solution.py:144
  421.1 5.8 collective-permute-start.8
  433.4 19.6 %psum.146 = f32[1]{0:T(128)} all-reduce(f32[1]{0:T(128)} %bitcast.74), channel_id=1, replica_groups=mesh['fx'=16,'fy'=8] {'fy'}, use_global_device_ids=true, to_apply=%region_18.19 | all-reduce | flops 1 | bytes 8 | tf_op jit(solution)/shard_map/psum | solution.py:144
  453.3 32.8 %psum.147 = f32[1]{0:T(128)} all-reduce(f32[1]{0:T(128)} %psum.146), channel_id=1, replica_groups=mesh['fx'=16,'fy'=8] {'fx'}, use_global_device_ids=true, to_apply=%region_19.20 | all-reduce | flops 1 | bytes 8 | tf_op jit(solution)/shard_map/psum | solution.py:144
  487.8 22.6 %psum.148 = f32[8,9]{0,1:T(8,128)S(1)} all-reduce(f32[8,9]{0,1:T(8,128)S(1)} %pad_maximum_fusion.17), channel_id=1, replica_groups=mesh['fx'=16,'fy'=8] {'fy'}, use_global_device_ids=true, to_apply=%region_20.21 | all-reduce | flops 72 | bytes 576 | tf_op jit(solution)/shard_map/psum | solution.py:144
  510.5 29.0 %psum.149 = f32[8,9]{0,1:T(8,128)S(1)} all-reduce(f32[8,9]{0,1:T(8,128)S(1)} %psum.148), channel_id=1, replica_groups=mesh['fx'=16,'fy'=8] {'fx'}, use_global_device_ids=true, to_apply=%region_21.22 | all-reduce | flops 72 | bytes 576 | tf_op jit(solution)/shard_map/psum | solution.py:144
  544.9 31.6 %convolution_bitcast_fusion.2 = f32[256,3,128]{2,1,0:T(4,128)} fusion(f32[256,2,3,128]{3,2,1,0:T(4,128)S(1)} %bitcast.472, f32[256,2,128,128]{3,2,1,0:T(8,128)} %bitcast.467), kind=kOutput, calls=%fused_computation.75 | convolution fusion | flops 301989888 | bytes 34734080 | tf_op jit(solution)/shard_map/gkij,gkcj->gci/dot_general | solution.py:120
  576.5 11.0 %all-to-all-start.4 = ((f32[256,3,128]{2,1,0:T(4,128)}), f32[256,3,128]{2,1,0:T(4,128)S(1)}, u32[]{:S(2)}, u32[]{:S(2)}) async-start(f32[256,3,128]{2,1,0:T(4,128)} %convolution_bitcast_fusion.2), calls=%async_computation.4 | async-start | bytes 1048576 | tf_op jit(solution)/shard_map/all_to_all | solution.py:140
  589.5 11.9 %all-to-all-done.4 = f32[256,3,128]{2,1,0:T(4,128)S(1)} async-done(((f32[256,3,128]{2,1,0:T(4,128)}), f32[256,3,128]{2,1,0:T(4,128)S(1)}, u32[]{:S(2)}, u32[]{:S(2)}) %all-to-all-start.4) | async-done | bytes 393248 | tf_op jit(solution)/shard_map/all_to_all | solution.py:140
  615.8 12.5 %scatter_fusion.2 = f32[256,3,128]{2,1,0:T(4,128)} fusion(f32[256,3,128]{2,1,0:T(4,128)} %broadcast.438, s32[128]{0:T(128)S(1)} %copy-done.27, f32[128,3,128]{2,1,0:T(4,128)S(1)} %copy.296), kind=kCustom, calls=%fused_computation.14 | custom fusion | bytes 590336 | tf_op jit(solution)/shard_map/scatter | solution.py:214
  628.3 4.5 all-to-all-start.5
  637.9 8.4 all-to-all-done.5
  646.3 19.6 %convolution_bitcast_fusion = f32[256,2,3,128]{3,2,1,0:T(4,128)S(1)} fusion(f32[256,2,128,128]{3,2,1,0:T(8,128)} %bitcast.468, f32[256,3,128]{2,1,0:T(4,128)S(1)} %all-to-all-done.5), kind=kOutput, calls=%fused_computation.73 | convolution fusion | flops 301989888 | bytes 34734080 | tf_op jit(solution)/shard_map/gkij,gci->gkcj/dot_general | solution.py:124
  672.6 19.0 %all-reduce.2 = (f32[1]{0:T(128)}, f32[1]{0:T(128)}) all-reduce(f32[1]{0:T(128)} %bitcast.119, f32[1]{0:T(128)} %bitcast.127), channel_id=1, replica_groups=mesh['fx'=16,'fy'=8] {'fy'}, use_global_device_ids=true, to_apply=%region_27.31 | all-reduce | flops 2 | bytes 16 | tf_op jit(solution)/shard_map/psum | solution.py:144
  691.6 32.7 %all-reduce = (f32[1]{0:T(128)}, f32[1]{0:T(128)}) all-reduce(f32[1]{0:T(128)} %get-tuple-element.198, f32[1]{0:T(128)} %get-tuple-element.199), channel_id=1, replica_groups=mesh['fx'=16,'fy'=8] {'fx'}, use_global_device_ids=true, to_apply=%region_28.32 | all-reduce | flops 2 | bytes 16 | tf_op jit(solution)/shard_map/psum | solution.py:144
  726.3 23.0 %psum.154 = f32[1]{0:T(128)} all-reduce(f32[1]{0:T(128)} %bitcast.129), channel_id=1, replica_groups=mesh['fx'=16,'fy'=8] {'fy'}, use_global_device_ids=true, to_apply=%region_33.37 | all-reduce | flops 1 | bytes 8 | tf_op jit(solution)/shard_map/psum | solution.py:144
  749.3 29.1 %psum.155 = f32[1]{0:T(128)} all-reduce(f32[1]{0:T(128)} %psum.154), channel_id=1, replica_groups=mesh['fx'=16,'fy'=8] {'fx'}, use_global_device_ids=true, to_apply=%region_34.38 | all-reduce | flops 1 | bytes 8 | tf_op jit(solution)/shard_map/psum | solution.py:144
  779.7 5.8 collective-permute-start.14
  792.0 19.5 %psum.156 = f32[1]{0:T(128)} all-reduce(f32[1]{0:T(128)} %bitcast.138), channel_id=1, replica_groups=mesh['fx'=16,'fy'=8] {'fy'}, use_global_device_ids=true, to_apply=%region_36.40 | all-reduce | flops 1 | bytes 8 | tf_op jit(solution)/shard_map/psum | solution.py:144
  811.6 32.7 %psum.157 = f32[1]{0:T(128)} all-reduce(f32[1]{0:T(128)} %psum.156), channel_id=1, replica_groups=mesh['fx'=16,'fy'=8] {'fx'}, use_global_device_ids=true, to_apply=%region_37.41 | all-reduce | flops 1 | bytes 8 | tf_op jit(solution)/shard_map/psum | solution.py:144
  846.3 22.6 %psum.158 = f32[8,9]{0,1:T(8,128)S(1)} all-reduce(f32[8,9]{0,1:T(8,128)S(1)} %pad_maximum_fusion.18), channel_id=1, replica_groups=mesh['fx'=16,'fy'=8] {'fy'}, use_global_device_ids=true, to_apply=%region_38.42 | all-reduce | flops 72 | bytes 576 | tf_op jit(solution)/shard_map/psum | solution.py:144
  869.0 29.0 %psum.159 = f32[8,9]{0,1:T(8,128)S(1)} all-reduce(f32[8,9]{0,1:T(8,128)S(1)} %psum.158), channel_id=1, replica_groups=mesh['fx'=16,'fy'=8] {'fx'}, use_global_device_ids=true, to_apply=%region_39.43 | all-reduce | flops 72 | bytes 576 | tf_op jit(solution)/shard_map/psum | solution.py:144
  (391 shorter events, 135.0 us)
Async XLA Ops:
  0.6 24.4 %copy-start = (f32[8,4,128,128]{3,2,1,0:T(8,128)S(1)}, f32[8,4,128,128]{3,2,1,0:T(8,128)}, u32[]{:S(2)}) copy-start(f32[8,4,128,128]{3,2,1,0:T(8,128)} %param.46) | copy-start | bytes 6291460
  0.6 27.7 %copy-start.1 = (f32[8,3,128]{2,0,1:T(8,128)S(1)}, f32[8,3,128]{2,0,1:T(8,128)}, u32[]{:S(2)}) copy-start(f32[8,3,128]{2,0,1:T(8,128)} %param.50) | copy-start | bytes 36868
  0.7 26.2 %copy-start.20 = (s32[8,4]{0,1:T(4,128)S(1)}, s32[8,4]{0,1:T(4,128)}, u32[]{:S(2)}) copy-start(s32[8,4]{0,1:T(4,128)} %param.47) | copy-start | bytes 388
  0.7 30.8 %copy-start.18 = (f32[128,3,128]{2,0,1:T(8,128)S(1)}, f32[128,3,128]{2,0,1:T(8,128)}, u32[]{:S(2)}) copy-start(f32[128,3,128]{2,0,1:T(8,128)} %param.41) | copy-start | bytes 589828
  1.7 29.9 %copy-start.25 = (f32[8,3,128]{2,0,1:T(8,128)S(1)}, f32[8,3,128]{2,0,1:T(8,128)}, u32[]{:S(2)}) copy-start(f32[8,3,128]{2,0,1:T(8,128)} %param.45) | copy-start | bytes 36868
  3.3 248.6 %copy-start.26 = (s32[128]{0:T(128)}, s32[128]{0:T(128)S(1)}, u32[]{:S(2)}) copy-start(s32[128]{0:T(128)S(1)} %fusion.166) | copy-start | bytes 1540
  6.5 38.6 %all-to-all-start = ((s32[128,2,2]{1,2,0:T(2,128)}), s32[128,2,2]{1,2,0:T(2,128)S(1)}, u32[]{:S(2)}, u32[]{:S(2)}) async-start(s32[128,2,2]{1,2,0:T(2,128)} %copy.261), calls=%async_computation | async-start | bytes 262144 | tf_op jit(solution)/shard_map/all_to_all | solution.py:134
  19.6 43.1 %collective-permute-start.1 = (f32[5,8,1,128]{3,1,2,0:T(8,128)}, f32[5,8,1,128]{3,1,2,0:T(8,128)S(1)}, u32[]{:S(2)}, u32[]{:S(2)}) collective-permute-start(f32[5,8,1,128]{3,1,2,0:T(8,128)} %bitcast.176), channel_id=1, source_target_pairs={{8,0},{16,8},{24,16},{32,24},{40,32},{48,40},{56,48},{64,56},{72,6... | collective-permute-start | bytes 61448 | tf_op jit(solution)/shard_map/ppermute | solution.py:27
  25.0 37.7 %collective-permute-start = (f32[5,8,1,128]{3,1,2,0:T(8,128)}, f32[5,8,1,128]{3,1,2,0:T(8,128)S(1)}, u32[]{:S(2)}, u32[]{:S(2)}) collective-permute-start(f32[5,8,1,128]{3,1,2,0:T(8,128)} %bitcast.175), channel_id=1, source_target_pairs={{0,8},{8,16},{16,24},{24,32},{32,40},{40,48},{48,56},{56,64},{64,7... | collective-permute-start | bytes 61448 | tf_op jit(solution)/shard_map/ppermute | solution.py:25
  27.7 278.8 %collective-permute-start.5 = (f32[8,3,128]{2,0,1:T(8,128)}, f32[8,3,128]{2,0,1:T(8,128)}, u32[]{:S(2)}, u32[]{:S(2)}) collective-permute-start(f32[8,3,128]{2,0,1:T(8,128)} %convolution_bitcast_fusion.22), channel_id=1, source_target_pairs={{1,0},{2,1},{3,2},{4,3},{5,4},{6,5},{7,6},{8,7},{9,8},{10,9},{11,1... | collective-permute-start | bytes 36872 | tf_op jit(solution)/shard_map/ppermute | solution.py:27
  28.3 245.5 %collective-permute-start.4 = (f32[8,3,128]{2,1,0:T(4,128)S(1)}, f32[8,3,128]{2,1,0:T(4,128)S(1)}, u32[]{:S(2)}, u32[]{:S(2)}) collective-permute-start(f32[8,3,128]{2,1,0:T(4,128)S(1)} %copy.275), channel_id=1, source_target_pairs={{0,1},{1,2},{2,3},{3,4},{4,5},{5,6},{6,7},{7,8},{8,9},{9,10},{10,1... | collective-permute-start | bytes 36872 | tf_op jit(solution)/shard_map/ppermute | solution.py:25
  30.7 29.7 %copy-start.9 = (f32[5,1,128,128]{3,2,1,0:T(8,128)}, f32[5,1,128,128]{3,2,1,0:T(8,128)S(1)}, u32[]{:S(2)}) copy-start(f32[5,1,128,128]{3,2,1,0:T(8,128)S(1)} %get-tuple-element.230) | copy-start | bytes 983044
  30.7 206.2 %copy-start.28 = (s32[1024]{0:T(1024)}, s32[1024]{0:T(1024)S(1)}, u32[]{:S(2)}) copy-start(s32[1024]{0:T(1024)S(1)} %pad_clamp_fusion.2) | copy-start | bytes 12292
  45.0 65.5 %all-to-all-start.1 = ((f32[256,3,128]{2,1,0:T(4,128)}), f32[256,3,128]{2,1,0:T(4,128)}, u32[]{:S(2)}, u32[]{:S(2)}) async-start(f32[256,3,128]{2,1,0:T(4,128)} %scatter_fusion), calls=%async_computation.1 | async-start | bytes 1048576 | tf_op jit(solution)/shard_map/all_to_all | solution.py:133
  64.7 4.2 copy-start.5
  73.4 13.5 %collective-permute-start.2 = (f32[5,8,130,1]{2,1,3,0:T(8,128)S(1)}, f32[5,8,130,1]{2,1,3,0:T(8,128)}, u32[]{:S(2)}, u32[]{:S(2)}) collective-permute-start(f32[5,8,130,1]{2,1,3,0:T(8,128)S(1)} %copy.253), channel_id=1, source_target_pairs={{0,1},{1,2},{2,3},{3,4},{4,5},{5,6},{6,7},{7,0},{8,9},{9,10},{10,1... | collective-permute-start | bytes 62408 | tf_op jit(solution)/shard_map/ppermute | solution.py:25
  78.9 2.7 copy-start.6
  78.9 11.2 %collective-permute-start.3 = (f32[5,8,130,1]{2,1,3,0:T(8,128)}, f32[5,8,130,1]{2,1,3,0:T(8,128)}, u32[]{:S(2)}, u32[]{:S(2)}) collective-permute-start(f32[5,8,130,1]{2,1,3,0:T(8,128)} %copy.254), channel_id=1, source_target_pairs={{1,0},{2,1},{3,2},{4,3},{5,4},{6,5},{7,6},{0,7},{9,8},{10,9},{11,1... | collective-permute-start | bytes 62408 | tf_op jit(solution)/shard_map/ppermute | solution.py:27
  81.7 1.1 copy-start.12
  82.7 1.7 copy-start.2
  213.7 23.2 %all-to-all-start.2 = ((f32[256,3,128]{2,1,0:T(4,128)}), f32[256,3,128]{2,1,0:T(4,128)}, u32[]{:S(2)}, u32[]{:S(2)}) async-start(f32[256,3,128]{2,1,0:T(4,128)} %convolution_bitcast_fusion.3), calls=%async_computation.2 | async-start | bytes 1048576 | tf_op jit(solution)/shard_map/all_to_all | solution.py:140
  223.9 14.8 %copy-start.14 = (f32[128,3,128]{2,0,1:T(8,128)S(1)}, f32[128,3,128]{2,0,1:T(8,128)}, u32[]{:S(2)}) copy-start(f32[128,3,128]{2,0,1:T(8,128)} %param.42) | copy-start | bytes 589828
  224.0 15.1 %copy-start.10 = (f32[5,1,128,128]{3,2,1,0:T(8,128)S(1)}, f32[5,1,128,128]{3,2,1,0:T(8,128)}, u32[]{:S(2)}) copy-start(f32[5,1,128,128]{3,2,1,0:T(8,128)} %copy-done.9) | copy-start | bytes 983044
  242.1 1.7 copy-start.3
  244.9 2.2 slice-start
  245.3 2.7 copy-start.7
  245.3 3.0 slice-start.1
  264.3 22.6 %all-to-all-start.3 = ((f32[256,3,128]{2,1,0:T(4,128)}), f32[256,3,128]{2,1,0:T(4,128)S(1)}, u32[]{:S(2)}, u32[]{:S(2)}) async-start(f32[256,3,128]{2,1,0:T(4,128)} %scatter_fusion.1), calls=%async_computation.3 | async-start | bytes 1048576 | tf_op jit(solution)/shard_map/all_to_all | solution.py:140
  273.8 32.7 %copy-start.23 = (s32[256,2]{0,1:T(2,128)}, s32[256,2]{0,1:T(2,128)S(1)}, u32[]{:S(2)}) copy-start(s32[256,2]{0,1:T(2,128)S(1)} %eq.26) | copy-start | bytes 6148
  276.2 30.3 %copy-start.19 = (f32[8,128]{1,0:T(8,128)S(1)}, f32[8,128]{1,0:T(8,128)}, u32[]{:S(2)}) copy-start(f32[8,128]{1,0:T(8,128)} %param.48) | copy-start | bytes 12292
  276.2 30.3 %copy-start.22 = (f32[8,3,128]{2,0,1:T(8,128)S(1)}, f32[8,3,128]{2,0,1:T(8,128)}, u32[]{:S(2)}) copy-start(f32[8,3,128]{2,0,1:T(8,128)} %param.49) | copy-start | bytes 36868
  307.7 2.5 collective-permute-start.6
  310.2 3.1 collective-permute-start.7
  312.6 140.4 %copy-start.16 = (f32[8,8,3,128]{3,1,2,0:T(8,128)S(1)}, f32[8,8,3,128]{3,1,2,0:T(8,128)}, u32[]{:S(2)}) copy-start(f32[8,8,3,128]{3,1,2,0:T(8,128)} %param.51) | copy-start | bytes 294916
  312.6 229.9 %copy-start.17 = (f32[8,8,3,128]{3,1,2,0:T(8,128)S(1)}, f32[8,8,3,128]{3,1,2,0:T(8,128)}, u32[]{:S(2)}) copy-start(f32[8,8,3,128]{3,1,2,0:T(8,128)} %param.52) | copy-start | bytes 294916
  421.1 9.2 %collective-permute-start.8 = (f32[8,3,128]{2,0,1:T(8,128)S(1)}, f32[8,3,128]{2,0,1:T(8,128)S(1)}, u32[]{:S(2)}, u32[]{:S(2)}) collective-permute-start(f32[8,3,128]{2,0,1:T(8,128)S(1)} %multiply_add_fusion.3), channel_id=1, source_target_pairs={{0,1},{1,2},{2,3},{3,4},{4,5},{5,6},{6,7},{7,8},{8,9},{9,10},{10,1... | collective-permute-start | bytes 36872 | tf_op jit(solution)/shard_map/ppermute | solution.py:25
  428.3 4.5 collective-permute-start.9
  576.5 24.9 %all-to-all-start.4 = ((f32[256,3,128]{2,1,0:T(4,128)}), f32[256,3,128]{2,1,0:T(4,128)S(1)}, u32[]{:S(2)}, u32[]{:S(2)}) async-start(f32[256,3,128]{2,1,0:T(4,128)} %convolution_bitcast_fusion.2), calls=%async_computation.4 | async-start | bytes 1048576 | tf_op jit(solution)/shard_map/all_to_all | solution.py:140
  587.6 47.9 %collective-permute-start.10 = (f32[8,3,128]{2,0,1:T(8,128)S(1)}, f32[8,3,128]{2,0,1:T(8,128)S(1)}, u32[]{:S(2)}, u32[]{:S(2)}) collective-permute-start(f32[8,3,128]{2,0,1:T(8,128)S(1)} %bitcast_subtract_fusion.1), channel_id=1, source_target_pairs={{0,1},{1,2},{2,3},{3,4},{4,5},{5,6},{6,7},{7,8},{8,9},{9,10},{10,1... | collective-permute-start | bytes 36872 | tf_op jit(solution)/shard_map/ppermute | solution.py:25
  607.2 1.7 copy-start.4
  607.2 1.8 copy-start.11
  610.4 1.7 copy-start.8
  612.2 2.6 copy-start.15
  612.2 3.7 copy-start.27
  613.3 1.5 copy-start.13
  628.3 18.0 %all-to-all-start.5 = ((f32[256,3,128]{2,1,0:T(4,128)}), f32[256,3,128]{2,1,0:T(4,128)S(1)}, u32[]{:S(2)}, u32[]{:S(2)}) async-start(f32[256,3,128]{2,1,0:T(4,128)} %scatter_fusion.2), calls=%async_computation.5 | async-start | bytes 1048576 | tf_op jit(solution)/shard_map/all_to_all | solution.py:140
  634.1 31.9 %collective-permute-start.11 = (f32[8,3,128]{2,0,1:T(8,128)S(1)}, f32[8,3,128]{2,0,1:T(8,128)S(1)}, u32[]{:S(2)}, u32[]{:S(2)}) collective-permute-start(f32[8,3,128]{2,0,1:T(8,128)S(1)} %convolution_bitcast_fusion.18), channel_id=1, source_target_pairs={{1,0},{2,1},{3,2},{4,3},{5,4},{6,5},{7,6},{8,7},{9,8},{10,9},{11,1... | collective-permute-start | bytes 36872 | tf_op jit(solution)/shard_map/ppermute | solution.py:27
  637.9 28.1 %copy-start.24 = (s32[256,2]{0,1:T(2,128)S(1)}, s32[256,2]{0,1:T(2,128)}, u32[]{:S(2)}) copy-start(s32[256,2]{0,1:T(2,128)} %copy-done.23) | copy-start | bytes 6148
  666.4 2.5 collective-permute-start.12
  668.9 3.1 collective-permute-start.13
  671.4 140.2 %slice-start.2 = ((f32[8,8,3,128]{3,1,2,0:T(8,128)}), f32[7,8,3,128]{3,1,2,0:T(8,128)S(1)}, s32[]{:S(2)}) async-start(f32[8,8,3,128]{3,1,2,0:T(8,128)} %param.51), calls=%async_computation.8 | async-start | bytes 172032 | tf_op jit(solution)/shard_map/slice | solution.py:247
  726.3 174.7 %slice-start.3 = ((f32[8,8,3,128]{3,1,2,0:T(8,128)}), f32[7,8,3,128]{3,1,2,0:T(8,128)S(1)}, s32[]{:S(2)}) async-start(f32[8,8,3,128]{3,1,2,0:T(8,128)} %param.52), calls=%async_computation.9 | async-start | bytes 172032 | tf_op jit(solution)/shard_map/slice | solution.py:249
  779.7 9.3 %collective-permute-start.14 = (f32[8,3,128]{2,0,1:T(8,128)S(1)}, f32[8,3,128]{2,0,1:T(8,128)S(1)}, u32[]{:S(2)}, u32[]{:S(2)}) collective-permute-start(f32[8,3,128]{2,0,1:T(8,128)S(1)} %multiply_add_fusion.1), channel_id=1, source_target_pairs={{0,1},{1,2},{2,3},{3,4},{4,5},{5,6},{6,7},{7,8},{8,9},{9,10},{10,1... | collective-permute-start | bytes 36872 | tf_op jit(solution)/shard_map/ppermute | solution.py:25
  786.8 4.6 collective-permute-start.15
  845.6 56.3 %copy-start.21 = (f32[8,3,128]{2,0,1:T(8,128)}, f32[8,3,128]{2,0,1:T(8,128)S(1)}, u32[]{:S(2)}) copy-start(f32[8,3,128]{2,0,1:T(8,128)S(1)} %get-tuple-element.205) | copy-start | bytes 36868
